TPU v7x, 32 devices: a whole 2x2x4 slice. The times are simulated.
32 devices in a mesh: dp: 8 (over y, x, core), mp: 4 (over z).
Axes of the slice: x: 2, y: 2, z: 4, core: 2. Of those that a mesh axis runs over, the one named last changes fastest.
Arguments:
- tokens: bfloat16 [20480, 1024], P(('dp', 'mp')), may hold values from -6 to 6
- context: int32 [40], P('dp'), may hold values from 0 to 475, as said below
- timestep: int32 [40], P('dp'), may hold values from 1 to 5000
- time_weight: float32 [1024], replicated, may hold values from -6 to 6
- time_bias: float32 [1024], replicated, may hold values from -3 to 3
- qkv_weight: bfloat16 [3, 1024, 1024], P(None, 'dp', 'mp'), may hold values from -0.1875 to 0.1875
- qv_bias: bfloat16 [16, 128], P('mp', 'dp'), may hold values from -3 to 3
- out_weight: bfloat16 [1024, 1024], P('mp', 'dp'), may hold values from -1 to 1
- out_bias: float32 [1024], replicated, may hold values from -3 to 3
- gain_one: float32 [1024], replicated, may hold values from 0.5 to 1.5
- shift_one: float32 [1024], replicated, may hold values from -3 to 3
- up_weight: bfloat16 [4096, 1024], P('mp', 'dp'), may hold values from -0.1875 to 0.1875
- up_bias: bfloat16 [32, 128], P('mp', 'dp'), may hold values from -3 to 3
- down_weight: bfloat16 [4096, 1024], P('mp', 'dp'), may hold values from -0.09375 to 0.09375
- down_bias: float32 [1024], replicated, may hold values from -3 to 3
- gain_two: float32 [1024], replicated, may hold values from 0.5 to 1.5
- shift_two: float32 [1024], replicated, may hold values from -3 to 3
- cotangent: bfloat16 [20480, 1024], P(('dp', 'mp')), may hold values from -6 to 6
Outputs:
- layer_out: bfloat16 [20480, 1024], P(('dp', 'mp'))
- grad_tokens: float32 [20480, 1024], P(('dp', 'mp'))
- grad_time_weight: float32 [1024], P(('dp', 'mp'))
- grad_time_bias: float32 [1024], P(('dp', 'mp'))
- grad_qkv_weight: float32 [3, 1024, 1024], P(None, 'dp', 'mp')
- grad_qv_bias: float32 [16, 128], P('mp', 'dp')
- grad_out_weight: float32 [1024, 1024], P('mp', 'dp')
- grad_out_bias: float32 [1024], P(('dp', 'mp'))
- grad_gain_one: float32 [1024], P(('dp', 'mp'))
- grad_shift_one: float32 [1024], P(('dp', 'mp'))
- grad_up_weight: float32 [4096, 1024], P('mp', 'dp')
- grad_up_bias: float32 [32, 128], P('mp', 'dp')
- grad_down_weight: float32 [4096, 1024], P('mp', 'dp')
- grad_down_bias: float32 [1024], P(('dp', 'mp'))
- grad_gain_two: float32 [1024], P(('dp', 'mp'))
- grad_shift_two: float32 [1024], P(('dp', 'mp'))
Inputs may be any that keep to these rules, and one draw needn't show every extreme that they name: Sequence b holds context[b] context tokens followed by 25 block tokens; its remaining positions are padding and are never attended to.
All inputs are finite; a program needn't handle non-finite values.
Results may differ from a plain program's by a relative error of at most 0.019.
Values may be sent and summed in bfloat16 or wider, within the bound.
A program may use at most 128 MiB of HBM per device.

v0:
```python
import math
import jax
import jax.numpy as jnp
from jax import lax
from jax.sharding import PartitionSpec as P

BLOCK = 25
TSTEPS = 5000
LN_EPS = 1e-05
MASKED = -1e30


def layer_norm(values_in, gain, shift):
    average = jnp.mean(values_in, axis=-1, keepdims=True)
    centred = values_in - average
    variance = jnp.mean(centred * centred, axis=-1, keepdims=True)
    return centred * lax.rsqrt(variance + LN_EPS) * gain + shift


def gelu_exact(values_in):
    return jax.nn.gelu(values_in, approximate=False)


def times_rows(left, right):
    return lax.dot_general(
        left, right, (((1,), (1,)), ((), ())), preferred_element_type=jnp.float32
    )


def times_cols(left, right):
    return lax.dot_general(
        left, right, (((0,), (0,)), ((), ())), preferred_element_type=jnp.float32
    )


def key_scores(queries, key_rows, live_len):
    head_size = queries.shape[-1]
    scores = jnp.einsum("qhd,khd->hqk", queries, key_rows, preferred_element_type=jnp.float32)
    scores = scores * (1.0 / math.sqrt(head_size))
    usable = jnp.arange(key_rows.shape[0]) < live_len
    return jnp.where(usable[None, None, :], scores, MASKED)


def forward_keys(key_count, record):
    seq_block, live_len = record
    queries = seq_block[:, 0]
    key_rows = seq_block[:key_count, 1]
    values = seq_block[:key_count, 2]
    scores = key_scores(queries, key_rows, live_len)
    row_max = jnp.max(scores, axis=-1, keepdims=True)
    expo_vals = jnp.exp(scores - row_max)
    total_e = jnp.sum(expo_vals, axis=-1, keepdims=True)
    prob_low = (expo_vals / total_e).astype(jnp.bfloat16)
    mixed_out = jnp.einsum("hqk,khd->qhd", prob_low, values, preferred_element_type=jnp.float32)
    return (mixed_out.astype(jnp.bfloat16), (row_max + jnp.log(total_e))[..., 0])


def backward_keys(key_count, record):
    seq_block, live_len, log_total, grad_out = record
    queries = seq_block[:, 0]
    key_rows = seq_block[:key_count, 1]
    values = seq_block[:key_count, 2]
    scale_factor = 1.0 / math.sqrt(queries.shape[-1])
    scores = key_scores(queries, key_rows, live_len)
    probs = jnp.exp(scores - log_total[..., None])
    grad_v = jnp.einsum(
        "hqk,qhd->khd", probs.astype(jnp.bfloat16), grad_out, preferred_element_type=jnp.float32
    )
    grad_p = jnp.einsum("qhd,khd->hqk", grad_out, values, preferred_element_type=jnp.float32)
    inner = jnp.sum(probs * grad_p, axis=-1, keepdims=True)
    grad_s = (probs * (grad_p - inner)).astype(jnp.bfloat16)
    grad_q = (
        jnp.einsum("hqk,khd->qhd", grad_s, key_rows, preferred_element_type=jnp.float32)
        * scale_factor
    )
    grad_k = (
        jnp.einsum("hqk,qhd->khd", grad_s, queries, preferred_element_type=jnp.float32)
        * scale_factor
    )
    return jnp.stack(
        [grad_q.astype(jnp.bfloat16), grad_k.astype(jnp.bfloat16), grad_v.astype(jnp.bfloat16)],
        axis=1,
    )


def body(
    tokens,
    context,
    timestep,
    time_weight,
    time_bias,
    qkv_weight,
    qv_bias,
    out_weight,
    out_bias,
    gain_one,
    shift_one,
    up_weight,
    up_bias,
    down_weight,
    down_bias,
    gain_two,
    shift_two,
    cotangent,
):
    mp_count = lax.axis_size("mp")
    mp_index = lax.axis_index("mp")
    shard_rows = tokens.shape[0]
    seq_count = context.shape[0]
    total_rows = shard_rows * mp_count
    seq_len = total_rows // seq_count
    qkv_weight, out_weight, qv_bias, up_weight, down_weight, up_bias = (
        lax.all_gather(qkv_weight, "dp", axis=1, tiled=True),
        lax.all_gather(out_weight, "dp", axis=1, tiled=True),
        lax.all_gather(qv_bias, "dp", axis=1, tiled=True),
        lax.all_gather(up_weight, "dp", axis=1, tiled=True),
        lax.all_gather(down_weight, "dp", axis=1, tiled=True),
        lax.all_gather(up_bias, "dp", axis=1, tiled=True),
    )
    local_width = qkv_weight.shape[2]
    local_heads = qv_bias.shape[0]
    head_size = qv_bias.shape[1] // 2
    row_ids = mp_index * shard_rows + jnp.arange(shard_rows, dtype=jnp.int32)
    owner = (row_ids // seq_len)[:, None] == jnp.arange(seq_count, dtype=jnp.int32)[None, :]
    frac_table = timestep.astype(jnp.float32) / TSTEPS
    fraction = jnp.sum(jnp.where(owner, frac_table[None, :], 0.0), axis=1)
    h_zero = tokens.astype(jnp.float32) + fraction[:, None] * time_weight + time_bias
    h_low = h_zero.astype(jnp.bfloat16)
    h_all = lax.all_gather(h_low, "mp", axis=0, tiled=True)
    bias_f = qv_bias.astype(jnp.float32)
    qkv_bias = jnp.stack(
        [
            bias_f[:, :head_size].reshape(local_width),
            jnp.zeros((local_width,), jnp.float32),
            bias_f[:, head_size:].reshape(local_width),
        ]
    )
    qkv_rows = (
        jnp.einsum("td,cde->tce", h_all, qkv_weight, preferred_element_type=jnp.float32) + qkv_bias
    ).astype(jnp.bfloat16)
    live_all = context + BLOCK
    seq_qkv = qkv_rows.reshape(seq_count, seq_len, 3, local_heads, head_size)
    mixed_seq, log_totals = lax.map(
        lambda record: forward_keys(seq_len, record), (seq_qkv, live_all)
    )
    attn_flat = mixed_seq.reshape(total_rows, local_width)
    branch_a = (
        lax.psum_scatter(
            jnp.dot(attn_flat, out_weight, preferred_element_type=jnp.float32),
            "mp",
            scatter_dimension=0,
            tiled=True,
        )
        + out_bias
    )
    y_one, ln_one_back = jax.vjp(layer_norm, h_zero + branch_a, gain_one, shift_one)
    y_low = y_one.astype(jnp.bfloat16)
    y_all = lax.all_gather(y_low, "mp", axis=0, tiled=True)
    pre_act = times_rows(y_all, up_weight) + up_bias.reshape(-1).astype(jnp.float32)
    hidden, gelu_back = jax.vjp(gelu_exact, pre_act)
    hidden_low = hidden.astype(jnp.bfloat16)
    branch_f = (
        lax.psum_scatter(
            jnp.dot(hidden_low, down_weight, preferred_element_type=jnp.float32).astype(
                jnp.bfloat16
            ),
            "mp",
            scatter_dimension=0,
            tiled=True,
        ).astype(jnp.float32)
        + down_bias
    )
    y_two, ln_two_back = jax.vjp(layer_norm, y_one + branch_f, gain_two, shift_two)
    layer_out = y_two.astype(jnp.bfloat16)
    grad_z2, grad_gain_two, grad_shift_two = ln_two_back(cotangent.astype(jnp.float32))
    grad_f_low = grad_z2.astype(jnp.bfloat16)
    grad_down_bias = jnp.sum(grad_f_low.astype(jnp.float32), axis=0)
    grad_f_all = lax.all_gather(grad_f_low, "mp", axis=0, tiled=True)
    (grad_pre,) = gelu_back(times_rows(grad_f_all, down_weight))
    grad_pre_low = grad_pre.astype(jnp.bfloat16)
    grad_up_weight = times_cols(grad_pre_low, y_all)
    grad_down_weight = times_cols(hidden_low, grad_f_all)
    grad_up_bias = jnp.sum(grad_pre_low.astype(jnp.float32), axis=0).reshape(up_bias.shape)
    grad_y1 = grad_z2 + lax.psum_scatter(
        jnp.dot(grad_pre_low, up_weight, preferred_element_type=jnp.float32).astype(jnp.bfloat16),
        "mp",
        scatter_dimension=0,
        tiled=True,
    ).astype(jnp.float32)
    grad_z1, grad_gain_one, grad_shift_one = ln_one_back(grad_y1)
    grad_a_low = grad_z1.astype(jnp.bfloat16)
    grad_out_bias = jnp.sum(grad_a_low.astype(jnp.float32), axis=0)
    grad_a_all = lax.all_gather(grad_a_low, "mp", axis=0, tiled=True)
    grad_attn = times_rows(grad_a_all, out_weight).astype(jnp.bfloat16)
    grad_out_weight = times_cols(attn_flat, grad_a_all)
    grad_seq = lax.map(
        lambda record: backward_keys(seq_len, record),
        (
            seq_qkv,
            live_all,
            log_totals,
            grad_attn.reshape(seq_count, seq_len, local_heads, head_size),
        ),
    )
    grad_qkv = grad_seq.reshape(total_rows, 3, local_width)
    grad_qkv_weight = jnp.einsum("td,tce->cde", h_all, grad_qkv, preferred_element_type=jnp.float32)
    bias_sums = jnp.sum(grad_qkv.astype(jnp.float32), axis=0)
    grad_qv_bias = jnp.concatenate(
        [
            bias_sums[0].reshape(local_heads, head_size),
            bias_sums[2].reshape(local_heads, head_size),
        ],
        axis=1,
    )
    grad_tokens = grad_z1 + lax.psum_scatter(
        jnp.einsum("tce,cde->td", grad_qkv, qkv_weight, preferred_element_type=jnp.float32).astype(
            jnp.bfloat16
        ),
        "mp",
        scatter_dimension=0,
        tiled=True,
    ).astype(jnp.float32)
    grad_time_weight = jnp.sum(fraction[:, None] * grad_tokens, axis=0)
    grad_time_bias = jnp.sum(grad_tokens, axis=0)
    (
        grad_qkv_weight,
        grad_out_weight,
        grad_qv_bias,
        grad_up_weight,
        grad_down_weight,
        grad_up_bias,
    ) = (
        lax.psum_scatter(grad_qkv_weight, "dp", scatter_dimension=1, tiled=True),
        lax.psum_scatter(grad_out_weight, "dp", scatter_dimension=1, tiled=True),
        lax.psum_scatter(grad_qv_bias, "dp", scatter_dimension=1, tiled=True),
        lax.psum_scatter(grad_up_weight, "dp", scatter_dimension=1, tiled=True),
        lax.psum_scatter(grad_down_weight, "dp", scatter_dimension=1, tiled=True),
        lax.psum_scatter(grad_up_bias, "dp", scatter_dimension=1, tiled=True),
    )
    (
        grad_out_bias,
        grad_gain_one,
        grad_shift_one,
        grad_gain_two,
        grad_shift_two,
        grad_down_bias,
        grad_time_weight,
        grad_time_bias,
    ) = (
        lax.psum_scatter(grad_out_bias, ("dp", "mp"), scatter_dimension=0, tiled=True),
        lax.psum_scatter(grad_gain_one, ("dp", "mp"), scatter_dimension=0, tiled=True),
        lax.psum_scatter(grad_shift_one, ("dp", "mp"), scatter_dimension=0, tiled=True),
        lax.psum_scatter(grad_gain_two, ("dp", "mp"), scatter_dimension=0, tiled=True),
        lax.psum_scatter(grad_shift_two, ("dp", "mp"), scatter_dimension=0, tiled=True),
        lax.psum_scatter(grad_down_bias, ("dp", "mp"), scatter_dimension=0, tiled=True),
        lax.psum_scatter(grad_time_weight, ("dp", "mp"), scatter_dimension=0, tiled=True),
        lax.psum_scatter(grad_time_bias, ("dp", "mp"), scatter_dimension=0, tiled=True),
    )
    return (
        layer_out,
        grad_tokens,
        grad_time_weight,
        grad_time_bias,
        grad_qkv_weight,
        grad_qv_bias,
        grad_out_weight,
        grad_out_bias,
        grad_gain_one,
        grad_shift_one,
        grad_up_weight,
        grad_up_bias,
        grad_down_weight,
        grad_down_bias,
        grad_gain_two,
        grad_shift_two,
    )


def solution(mesh):
    placed = (
        P(("dp", "mp"), None),
        P("dp"),
        P("dp"),
        P(),
        P(),
        P(None, "dp", "mp"),
        P("mp", "dp"),
        P("mp", "dp"),
        P(),
        P(),
        P(),
        P("mp", "dp"),
        P("mp", "dp"),
        P("mp", "dp"),
        P(),
        P(),
        P(),
        P(("dp", "mp"), None),
    )
    return jax.shard_map(
        body,
        mesh=mesh,
        in_specs=placed,
        out_specs=(
            P(("dp", "mp"), None),
            P(("dp", "mp"), None),
            P(("dp", "mp")),
            P(("dp", "mp")),
            P(None, "dp", "mp"),
            P("mp", "dp"),
            P("mp", "dp"),
            P(("dp", "mp")),
            P(("dp", "mp")),
            P(("dp", "mp")),
            P("mp", "dp"),
            P("mp", "dp"),
            P("mp", "dp"),
            P(("dp", "mp")),
            P(("dp", "mp")),
            P(("dp", "mp")),
        ),
        check_vma=False,
    )
```

profile of v0, /device:TPU:0, one launch (start us, length us, event | category | flops | bytes accessed | tf_op | source)
XLA Modules:
  0.0 1414.3 jit_solution(10360146816921266265)
XLA Ops:
  8.8 2.8 fusion.47
  11.7 10.6 all-gather
  22.7 9.8 all_gather.33
  32.5 5.7 all-gather.12.cloned.1.call-done
  38.2 100.2 %all-gather.10.cloned.1.call-done = bf16[2560,1024]{1,0:T(8,128)(2,1)} async-done(((bf16[640,1024]{1,0:T(8,128)(2,1)}), bf16[2560,1024]{1,0:T(8,128)(2,1)}) %all-gather.10.cloned.1.call-update) | async-done | bytes 5242896 | tf_op jit(solution)/shard_map/all_gather | solution.py:129
  138.4 9.2 add_convert_fusion.1
  147.6 12.2 reshape.203
  159.9 12.0 copy.94
  171.9 31.1 %while.22 = (s32[]{:T(128)}, bf16[5,512,4,64]{1,3,2,0:T(8,128)(2,1)S(1)}, f32[5,4,512]{2,1,0:T(4,128)}, bf16[5,512,3,4,64]{1,4,3,2,0:T(8,128)(2,1)}, s32[5]{0:T(128)S(1)}, /*index=5*/s32[]{:T(128)}) while((s32[]{:T(128)}, bf16[5,512,4,64]{1,3,2,0:T(8,128)(2,1)S(1)}, f32[5,4,512]{2,1,0:T(4,128)}, bf16[5,512,3,4,64]{1,4,3,2,0:T(8,128)(2,1)}, ...), condition=%wide.region_4.5_spmd, body=%wide.region_1.4_spmd.sunk | while | flops 281147904 | bytes 15272541 | solution.py:143
  205.5 5.6 fusion.65
  212.2 175.4 %reduce-scatter.15.cloned.1.call-done = f32[640,1024]{1,0:T(8,128)} async-done(((f32[2560,1024]{1,0:T(8,128)}), f32[640,1024]{1,0:T(8,128)}) %reduce-scatter.15.cloned.1.call-update) | async-done | bytes 2621456 | tf_op jit(solution)/shard_map/reduce_scatter | solution.py:148
  387.7 2.9 fusion.63
  391.0 1.5 fusion.48
  393.2 8.9 all-gather.1
  402.2 16.4 %all-gather.16.cloned.1.call-done = bf16[1024,1024]{1,0:T(8,128)(2,1)} async-done(((bf16[1024,128]{1,0:T(8,128)(2,1)}), bf16[1024,1024]{1,0:T(8,128)(2,1)}) %all-gather.16.cloned.1.call-update) | async-done | bytes 2097168 | tf_op jit(solution)/shard_map/all_gather | solution.py:116
  418.6 100.1 %all-gather.14.cloned.1.call-done = bf16[2560,1024]{1,0:T(8,128)(2,1)} async-done(((bf16[640,1024]{1,0:T(8,128)(2,1)}), bf16[2560,1024]{1,0:T(8,128)(2,1)}) %all-gather.14.cloned.1.call-update) | async-done | bytes 5242896 | tf_op jit(solution)/shard_map/all_gather | solution.py:158
  518.6 32.1 %multiply_convert_fusion.1 = (bf16[2560,1024]{1,0:T(8,128)(2,1)}, f32[2560,1024]{1,0:T(8,128)}, f32[2560,1024]{1,0:T(8,128)}) fusion(f32[1024]{0:T(1024)S(1)} %bitcast.187, bf16[2560,1024]{1,0:T(8,128)(2,1)} %all-gather.14.cloned.1.call-done, bf16[1024,1024]{1,0:T(8,128)(2,1)} %all-gather.16.cloned.1.call-done), kind=kOutput, calls=%fused_computation.55 | convolution fusion | flops 5541724160 | bytes 33558528 | tf_op jit(solution)/shard_map/dot_general | solution.py:25
  550.8 10.2 convolution_convert_fusion.1
  561.3 92.0 %reduce-scatter.17.cloned.1.call-done = bf16[640,1024]{1,0:T(8,128)(2,1)} async-done(((bf16[2560,1024]{1,0:T(8,128)(2,1)}), bf16[640,1024]{1,0:T(8,128)(2,1)}) %reduce-scatter.17.cloned.1.call-update) | async-done | bytes 1310736 | tf_op jit(solution)/shard_map/reduce_scatter | solution.py:163
  653.3 2.3 fusion.61
  656.1 1.5 fusion.46
  657.6 2.1 fusion.60
  659.8 1.5 copy-done
  661.3 1.9 convert_reduce_fusion.3
  663.3 98.6 %all-gather.20.cloned.1.call-done = bf16[2560,1024]{1,0:T(8,128)(2,1)} async-done(((bf16[640,1024]{1,0:T(8,128)(2,1)}), bf16[2560,1024]{1,0:T(8,128)(2,1)}) %all-gather.20.cloned.1.call-update) | async-done | bytes 5242896 | tf_op jit(solution)/shard_map/all_gather | solution.py:178
  761.9 16.5 %convert_reduce_fusion = (f32[1024]{0:T(1024)S(1)}, bf16[2560,1024]{1,0:T(8,128)(2,1)S(1)}) fusion(f32[2560,1024]{1,0:T(8,128)} %get-tuple-element.266, f32[2560,1024]{1,0:T(8,128)} %get-tuple-element.278, f32[1024]{0:T(1024)S(1)} %bitcast.188, bf16[2560,1024]{1,0:T(8,128)(2,1)} %all-gather.20.cloned.1.call-done, ...), kind=kOutput, calls=%fused_computation.53 | convolution fusion | flops 5413272576 | bytes 33562624 | tf_op jit(solution)/shard_map/dot_general | solution.py:25
  778.5 2.4 copy-done.27
  780.9 7.3 convolution_convert_fusion
  788.2 92.2 %reduce-scatter.19.cloned.1.call-done = bf16[640,1024]{1,0:T(8,128)(2,1)} async-done(((bf16[2560,1024]{1,0:T(8,128)(2,1)}), bf16[640,1024]{1,0:T(8,128)(2,1)}) %reduce-scatter.19.cloned.1.call-update) | async-done | bytes 1310736 | tf_op jit(solution)/shard_map/reduce_scatter | solution.py:184
  880.5 3.5 multiply_reduce_fusion.1
  885.2 1.5 copy-done.2
  888.9 97.8 %all-gather.22.cloned.1.call-done = bf16[2560,1024]{1,0:T(8,128)(2,1)} async-done(((bf16[640,1024]{1,0:T(8,128)(2,1)}), bf16[2560,1024]{1,0:T(8,128)(2,1)}) %all-gather.22.cloned.1.call-update) | async-done | bytes 5242896 | tf_op jit(solution)/shard_map/all_gather | solution.py:193
  986.7 5.1 convolution_convert_fusion.2
  991.8 4.2 reshape.198
  996.1 3.0 copy.99
  999.1 60.0 %while.23 = (s32[]{:T(128)}, bf16[5,512,3,4,64]{1,4,3,2,0:T(8,128)(2,1)}, bf16[5,512,3,4,64]{1,4,3,2,0:T(8,128)(2,1)}, s32[5]{0:T(128)S(1)}, f32[5,4,512]{2,1,0:...) while((s32[]{:T(128)}, bf16[5,512,3,4,64]{1,4,3,2,0:T(8,128)(2,1)}, ...), condition=%wide.region_18.19_spmd, body=%wide.region_16.18_spmd.sunk | while | flops 689830400 | bytes 37285476 | solution.py:196
  1003.0 2.4 multiply_reduce_fusion.7
  1008.0 2.1 fusion.113
  1015.0 2.4 multiply_reduce_fusion.7
  1020.0 2.1 fusion.113
  1027.0 2.4 multiply_reduce_fusion.7
  1029.4 1.4 multiply_convert_fusion.3
  1032.0 2.1 fusion.113
  1039.0 2.4 multiply_reduce_fusion.7
  1041.4 1.4 multiply_convert_fusion.3
  1044.0 2.1 fusion.113
  1051.0 2.4 multiply_reduce_fusion.7
  1056.0 2.1 fusion.113
  1059.1 2.7 convert_reduce_fusion.1
  1061.9 7.7 copy.100
  1070.3 9.7 reshape.187
  1080.3 9.7 fusion.49
  1090.0 8.3 bitcast_convert_fusion
  1098.4 10.5 fusion.68
  1108.9 10.5 fusion.67
  1119.5 5.9 fusion.66
  1128.2 33.3 %reduce-scatter.23.cloned.1.call-done = f32[3,128,256]{1,2,0:T(8,128)} async-done(((f32[3,1024,256]{1,2,0:T(8,128)}), f32[3,128,256]{1,2,0:T(8,128)}) %reduce-scatter.23.cloned.1.call-update) | async-done | bytes 393232 | tf_op jit(solution)/shard_map/reduce_scatter | solution.py:233
  1161.5 1.9 copy.102
  1163.4 94.1 %reduce-scatter.21.cloned.1.call-done = bf16[640,1024]{1,0:T(8,128)(2,1)} async-done(((bf16[2560,1024]{1,0:T(8,128)(2,1)}), bf16[640,1024]{1,0:T(8,128)(2,1)}) %reduce-scatter.21.cloned.1.call-update) | async-done | bytes 1310736 | tf_op jit(solution)/shard_map/reduce_scatter | solution.py:215
  1257.5 3.4 fusion.58
  1260.9 41.5 %all-reduce.8 = (f32[1024]{0:T(1024)S(1)}, f32[1024]{0:T(1024)S(1)}, f32[1024]{0:T(1024)S(1)}, f32[1024]{0:T(1024)S(1)}, f32[1024]{0:T(1024)S(1)}, /*index=5*/f3...) all-reduce(f32[1024]{0:T(1024)S(1)} %get-tuple-element.220, ...), channel_id=6, replica_groups=mesh['dp'=8,'mp'=4] {'dp','mp'}, use_global_device_ids=true, to_apply=%region_21.22.clone | all-reduce | flops 8192 | bytes 65536
  1307.1 6.0 reduce-scatter.29.cloned.1.call-done
  1313.1 54.8 %reduce-scatter.27.cloned.1.call-done = f32[1024,128]{1,0:T(8,128)} async-done(((f32[1024,1024]{1,0:T(8,128)}), f32[1024,128]{1,0:T(8,128)}) %reduce-scatter.27.cloned.1.call-update) | async-done | bytes 524304 | tf_op jit(solution)/shard_map/reduce_scatter | solution.py:236
  1367.9 39.6 %reduce-scatter.25.cloned.1.call-done = f32[256,128]{1,0:T(8,128)} async-done(((f32[256,1024]{1,0:T(8,128)}), f32[256,128]{1,0:T(8,128)}) %reduce-scatter.25.cloned.1.call-update) | async-done | bytes 131088 | tf_op jit(solution)/shard_map/reduce_scatter | solution.py:234
  (212 shorter events, 85.1 us)
Async XLA Ops:
  7.2 15.5 %copy-start.7 = (bf16[256,128]{1,0:T(8,128)(2,1)S(1)}, bf16[256,128]{1,0:T(8,128)(2,1)}, u32[]{:S(2)}) copy-start(bf16[256,128]{1,0:T(8,128)(2,1)} %param.29) | copy-start | bytes 196612
  7.2 25.3 %copy-start.24 = (s32[5]{0:T(128)S(1)}, s32[5]{0:T(128)}, u32[]{:S(2)}) copy-start(s32[5]{0:T(128)} %param.23) | copy-start | bytes 64
  7.2 31.0 %all-gather.12.cloned.1.call-start = ((), (), s32[]{:S(2)}) async-start(), calls=%async_computation.11 | async-start | bytes 1769472 | tf_op jit(solution)/shard_map/all_gather | solution.py:113
  7.9 130.5 %all-gather.10.cloned.1.call-start = ((), (), s32[]{:S(2)}) async-start(), calls=%async_computation.10 | async-start | bytes 6553600 | tf_op jit(solution)/shard_map/all_gather | solution.py:129
  8.7 378.9 %copy-start.8 = (f32[640]{0:T(1024)}, f32[640]{0:T(1024)S(1)}, u32[]{:S(2)}) copy-start(f32[640]{0:T(1024)S(1)} %select_reduce_fusion) | copy-start | bytes 7684
  11.6 376.0 %reduce-scatter.15.cloned.1.call-start = ((), (), s32[]{:S(2)}) async-start(), calls=%async_computation.12 | async-start | bytes 13107200 | tf_op jit(solution)/shard_map/reduce_scatter | solution.py:148
  203.0 8.0 copy-start.25
  204.5 1.1 copy-start.4
  211.1 176.6 %copy-start.11 = (f32[1024]{0:T(1024)S(1)}, f32[1024]{0:T(1024)}, u32[]{:S(2)}) copy-start(f32[1024]{0:T(1024)} %param.26) | copy-start | bytes 12292
  211.1 176.6 %copy-start.12 = (f32[1024]{0:T(1024)S(1)}, f32[1024]{0:T(1024)}, u32[]{:S(2)}) copy-start(f32[1024]{0:T(1024)} %param.25) | copy-start | bytes 12292
  211.1 176.6 %copy-start.20 = (f32[1024]{0:T(1024)S(1)}, f32[1024]{0:T(1024)}, u32[]{:S(2)}) copy-start(f32[1024]{0:T(1024)} %param.30) | copy-start | bytes 12292
  211.1 207.5 %all-gather.16.cloned.1.call-start = ((), (), s32[]{:S(2)}) async-start(), calls=%async_computation.14 | async-start | bytes 2359296 | tf_op jit(solution)/shard_map/all_gather | solution.py:116
  211.7 179.3 %copy-start.10 = (f32[1024]{0:T(1024)S(1)}, f32[1024]{0:T(1024)}, u32[]{:S(2)}) copy-start(f32[1024]{0:T(1024)} %param.31) | copy-start | bytes 12292
  211.7 179.3 %copy-start.13 = (f32[1024]{0:T(1024)S(1)}, f32[1024]{0:T(1024)}, u32[]{:S(2)}) copy-start(f32[1024]{0:T(1024)} %param.32) | copy-start | bytes 12292
  211.7 306.9 %all-gather.14.cloned.1.call-start = ((), (), s32[]{:S(2)}) async-start(), calls=%async_computation.13 | async-start | bytes 6553600 | tf_op jit(solution)/shard_map/all_gather | solution.py:158
  390.6 2.6 copy-start.21
  392.6 158.2 %all-gather.18.cloned.1.call-start = ((), (), s32[]{:S(2)}) async-start(), calls=%async_computation.15 | async-start | bytes 2359296 | tf_op jit(solution)/shard_map/all_gather | solution.py:117
  393.2 260.2 %reduce-scatter.17.cloned.1.call-start = ((), (), s32[]{:S(2)}) async-start(), calls=%async_computation.16 | async-start | bytes 6553600 | tf_op jit(solution)/shard_map/reduce_scatter | solution.py:163
  561.0 92.3 %copy-start.18 = (f32[1024]{0:T(1024)S(1)}, f32[1024]{0:T(1024)}, u32[]{:S(2)}) copy-start(f32[1024]{0:T(1024)} %param.36) | copy-start | bytes 12292
  561.0 95.1 %copy-start.14 = (f32[1024]{0:T(1024)S(1)}, f32[1024]{0:T(1024)}, u32[]{:S(2)}) copy-start(f32[1024]{0:T(1024)} %param.37) | copy-start | bytes 12292
  561.1 200.9 %all-gather.20.cloned.1.call-start = ((), (), s32[]{:S(2)}) async-start(), calls=%async_computation.17 | async-start | bytes 6553600 | tf_op jit(solution)/shard_map/all_gather | solution.py:178
  653.3 2.8 copy-start.5
  655.7 1.9 copy-start.19
  659.8 1.5 copy-start
  663.2 217.2 %reduce-scatter.19.cloned.1.call-start = ((), (), s32[]{:S(2)}) async-start(), calls=%async_computation.18 | async-start | bytes 6553600 | tf_op jit(solution)/shard_map/reduce_scatter | solution.py:184
  761.9 19.0 %copy-start.22 = (bf16[1024,1024]{1,0:T(8,128)(2,1)S(1)}, bf16[1024,1024]{1,0:T(8,128)(2,1)}, u32[]{:S(2)}) copy-start(bf16[1024,1024]{1,0:T(8,128)(2,1)} %all-gather.16.cloned.1.call-done) | copy-start | bytes 6291460
  778.5 2.4 copy-start.27
  788.2 198.5 %all-gather.22.cloned.1.call-start = ((), (), s32[]{:S(2)}) async-start(), calls=%async_computation.19 | async-start | bytes 6553600 | tf_op jit(solution)/shard_map/all_gather | solution.py:193
  880.5 3.5 copy-start.1
  880.5 3.5 copy-start.6
  885.1 1.5 copy-start.2
  888.0 237.5 %reduce-scatter.33.cloned.1.call-start = ((), (), s32[]{:S(2)}) async-start(), calls=%async_computation.26 | async-start | bytes 73728
  888.8 238.0 %reduce-scatter.31.cloned.1.call-start = ((), (), s32[]{:S(2)}) async-start(), calls=%async_computation.25 | async-start | bytes 73728
  991.8 7.3 copy-start.26
  1080.1 10.0 copy-start.23
  1080.1 81.5 %reduce-scatter.23.cloned.1.call-start = ((), (), s32[]{:S(2)}) async-start(), calls=%async_computation.21 | async-start | bytes 3538944 | tf_op jit(solution)/shard_map/reduce_scatter | solution.py:233
  1090.0 167.5 %reduce-scatter.21.cloned.1.call-start = ((), (), s32[]{:S(2)}) async-start(), calls=%async_computation.20 | async-start | bytes 6553600 | tf_op jit(solution)/shard_map/reduce_scatter | solution.py:215
  1098.3 214.8 %reduce-scatter.29.cloned.1.call-start = ((), (), s32[]{:S(2)}) async-start(), calls=%async_computation.24 | async-start | bytes 4718592 | tf_op jit(solution)/shard_map/reduce_scatter | solution.py:237
  1108.9 259.1 %reduce-scatter.27.cloned.1.call-start = ((), (), s32[]{:S(2)}) async-start(), calls=%async_computation.23 | async-start | bytes 4718592 | tf_op jit(solution)/shard_map/reduce_scatter | solution.py:236
  1119.4 138.1 %copy-start.3 = (f32[640,1024]{1,0:T(8,128)S(1)}, f32[640,1024]{1,0:T(8,128)}, u32[]{:S(2)}) copy-start(f32[640,1024]{1,0:T(8,128)} %copy-done.2) | copy-start | bytes 7864324
  1119.5 138.1 %copy-start.9 = (f32[640]{0:T(1024)S(1)}, f32[640]{0:T(1024)}, u32[]{:S(2)}) copy-start(f32[640]{0:T(1024)} %copy-done.8) | copy-start | bytes 7684
  1119.5 288.1 %reduce-scatter.25.cloned.1.call-start = ((), (), s32[]{:S(2)}) async-start(), calls=%async_computation.22 | async-start | bytes 1179648 | tf_op jit(solution)/shard_map/reduce_scatter | solution.py:234
  1125.4 135.5 %copy-start.15 = (f32[1024]{0:T(1024)S(1)}, f32[1024]{0:T(1024)}, u32[]{:S(2)}) copy-start(f32[1024]{0:T(1024)} %get-tuple-element.216) | copy-start | bytes 12292
  1125.4 135.5 %copy-start.16 = (f32[1024]{0:T(1024)S(1)}, f32[1024]{0:T(1024)}, u32[]{:S(2)}) copy-start(f32[1024]{0:T(1024)} %get-tuple-element.221) | copy-start | bytes 12292
  1125.4 135.5 %copy-start.17 = (f32[1024]{0:T(1024)S(1)}, f32[1024]{0:T(1024)}, u32[]{:S(2)}) copy-start(f32[1024]{0:T(1024)} %get-tuple-element.254) | copy-start | bytes 12292
Sparse Core Ops, SparseCore 0:
  9.9 28.2 all-gather.11
  40.4 98.0 all-gather.9
  211.2 176.3 reduce-scatter.14
  389.4 29.1 all-gather.15
  420.6 98.0 all-gather.13
  520.4 26.4 all-gather.17
  561.2 92.1 reduce-scatter.16
  663.3 98.5 all-gather.19
  788.3 92.0 reduce-scatter.18
  888.1 98.5 all-gather.21
  989.7 31.9 reduce-scatter.32
  1080.2 31.8 reduce-scatter.30
  1115.4 46.0 reduce-scatter.22
  1163.7 93.7 reduce-scatter.20
  1261.3 51.7 reduce-scatter.28
  1316.9 51.0 reduce-scatter.26
  1371.5 35.9 reduce-scatter.24
where the time goes:
time: 1430 us; the launch traced here: 1410 us
  waiting for transfers between devices  1010 us (71%)
  matrix products  175 us (12%)
  local copies, waits for them, and re-layouts  89.3 us (6%)
  blocking collectives  70.7 us (5%)
  other arithmetic  55 us (4%)
  between operations  14.5 us (1%)
    reduce_scatter x1, waiting for transfers between devices, body(): lax.psum_scatter(jnp.dot(attn_flat, out_weight, preferred_element_type=jn...  175 us
    all_gather x1, waiting for transfers between devices, body(): h_all = lax.all_gather(h_low, 'mp', axis=0, tiled=True)  100 us
    all_gather x1, waiting for transfers between devices, body(): y_all = lax.all_gather(y_low, 'mp', axis=0, tiled=True)  100 us
    all_gather x1, waiting for transfers between devices, body(): grad_f_all = lax.all_gather(grad_f_low, 'mp', axis=0, tiled=True)  98.6 us
    all_gather x1, waiting for transfers between devices, body(): grad_a_all = lax.all_gather(grad_a_low, 'mp', axis=0, tiled=True)  97.8 us
    reduce_scatter x1, waiting for transfers between devices, body(): lax.psum_scatter(jnp.einsum('tce,cde->td', grad_qkv, qkv_weight, preferre...  94.1 us
    reduce_scatter x1, waiting for transfers between devices, body(): lax.psum_scatter(jnp.dot(grad_pre_low, up_weight, preferred_element_type=...  92.2 us
    reduce_scatter x1, waiting for transfers between devices, body(): lax.psum_scatter(jnp.dot(hidden_low, down_weight, preferred_element_type=...  92 us
  transfers between devices with their start and end apart: 17, of which 14 were waited for; matrix products, arithmetic and copies ran while one was open for 14% of the time, Pallas kernels for 0%

commit v1 on v0

--- a/solution.py
+++ b/solution.py
@@ -8,6 +8,12 @@
 TSTEPS = 5000
 LN_EPS = 1e-05
 MASKED = -1e30
+
+
+def laid_out(blocks, dim):
+    dims = list(blocks.shape[1:])
+    dims[dim] *= blocks.shape[0]
+    return jnp.moveaxis(blocks, 0, dim).reshape(dims)
 
 
 def layer_norm(values_in, gain, shift):
@@ -126,7 +132,19 @@
     fraction = jnp.sum(jnp.where(owner, frac_table[None, :], 0.0), axis=1)
     h_zero = tokens.astype(jnp.float32) + fraction[:, None] * time_weight + time_bias
     h_low = h_zero.astype(jnp.bfloat16)
-    h_all = lax.all_gather(h_low, "mp", axis=0, tiled=True)
+    size = lax.axis_size("mp")
+    pairs = [(i, (i + 1) % size) for i in range(size)]
+    back = [(b, a) for a, b in pairs]
+    lower, upper = ([], [])
+    for step in range(size - 1):
+        if step % 2 == 0:
+            lower.append(lax.ppermute(lower[-1] if lower else h_low, "mp", pairs))
+        else:
+            upper.append(lax.ppermute(upper[-1] if upper else h_low, "mp", back))
+    tiles = jnp.stack([*lower[::-1], h_low, *upper])
+    offset = lax.axis_index("mp") - len(lower)
+    tiles = tiles[(jnp.arange(size) - offset) % size]
+    h_all = laid_out(tiles, 0)
     bias_f = qv_bias.astype(jnp.float32)
     qkv_bias = jnp.stack(
         [

time: 1430 us -> 1400 us (0.979)
  waiting for transfers between devices: 1010 us -> 966 us
    all_gather x1 -> x0, waiting for transfers between devices: 100 us -> none  [body(): h_all = lax.all_gather(h_low, 'mp', axis=0, tiled=True)]
    ppermute x0 -> x3, waiting for transfers between devices: none -> 63.1 us  [the longest x2 48.7 us: body(): lower.append(lax.ppermute(lower[-1] if lower else h_low, 'mp', pairs))]
  transfers between devices with their start and end apart: 17 -> 19, of which waited for: 14 -> 15; matrix products, arithmetic and copies ran while one was open for 14% -> 14% of each run, Pallas kernels for 0% -> 0%
where the time goes in v1:
time: 1400 us; the launch traced here: 1390 us
  waiting for transfers between devices  966 us (69%)
  matrix products  175 us (12%)
  local copies, waits for them, and re-layouts  95.2 us (7%)
  blocking collectives  70.2 us (5%)
  other arithmetic  61.5 us (4%)
  between operations  14.5 us (1%)
    reduce_scatter x1, waiting for transfers between devices, body(): lax.psum_scatter(jnp.dot(attn_flat, out_weight, preferred_element_type=jn...  177 us
    all_gather x1, waiting for transfers between devices, body(): y_all = lax.all_gather(y_low, 'mp', axis=0, tiled=True)  100 us
    all_gather x1, waiting for transfers between devices, body(): grad_f_all = lax.all_gather(grad_f_low, 'mp', axis=0, tiled=True)  98.7 us
    all_gather x1, waiting for transfers between devices, body(): grad_a_all = lax.all_gather(grad_a_low, 'mp', axis=0, tiled=True)  97.8 us
    reduce_scatter x1, waiting for transfers between devices, body(): lax.psum_scatter(jnp.einsum('tce,cde->td', grad_qkv, qkv_weight, preferre...  94.2 us
    reduce_scatter x1, waiting for transfers between devices, body(): lax.psum_scatter(jnp.dot(grad_pre_low, up_weight, preferred_element_type=...  92.2 us
    reduce_scatter x1, waiting for transfers between devices, body(): lax.psum_scatter(jnp.dot(hidden_low, down_weight, preferred_element_type=...  92 us
    reduce_scatter x1, waiting for transfers between devices, body(): lax.psum_scatter(grad_up_weight, 'dp', scatter_dimension=1, tiled=True)  54.8 us
  transfers between devices with their start and end apart: 19, of which 15 were waited for; matrix products, arithmetic and copies ran while one was open for 14% of the time, Pallas kernels for 0%

profile of v1, /device:TPU:0, one launch (start us, length us, event | category | flops | bytes accessed | tf_op | source)
XLA Modules:
  0.0 1388.8 jit_solution(13122092676789800500)
XLA Ops:
  8.1 2.8 fusion.44
  10.9 3.1 collective-permute-start
  14.1 2.1 collective-permute-start.2
  16.2 9.3 all-gather
  25.4 20.5 %collective-permute-done = bf16[640,1024]{1,0:T(8,128)(2,1)S(1)} collective-permute-done((bf16[640,1024]{1,0:T(8,128)(2,1)}, bf16[640,1024]{1,0:T(8,128)(2,1)S(1)}, u32[]{:S(2)}, u32[]{:S(2)}) %collective-permute-start) | collective-permute-done | bytes 1310752 | tf_op jit(solution)/shard_map/ppermute | solution.py:141
  46.3 10.5 all_gather.29
  58.7 14.4 %collective-permute-done.2 = bf16[640,1024]{1,0:T(8,128)(2,1)} collective-permute-done((bf16[640,1024]{1,0:T(8,128)(2,1)}, bf16[640,1024]{1,0:T(8,128)(2,1)}, u32[]{:S(2)}, u32[]{:S(2)}) %collective-permute-start.2) | collective-permute-done | bytes 1310752 | tf_op jit(solution)/shard_map/ppermute | solution.py:143
  73.1 28.2 %collective-permute-done.1 = bf16[640,1024]{1,0:T(8,128)(2,1)} collective-permute-done((bf16[640,1024]{1,0:T(8,128)(2,1)S(1)}, bf16[640,1024]{1,0:T(8,128)(2,1)}, u32[]{:S(2)}, u32[]{:S(2)}) %collective-permute-start.1) | collective-permute-done | bytes 1310752 | tf_op jit(solution)/shard_map/ppermute | solution.py:141
  101.3 4.6 pad_maximum_fusion
  106.0 5.7 gather_fusion
  111.7 9.2 add_convert_fusion.1
  120.9 12.2 reshape.264
  133.1 12.1 copy.94
  145.2 31.1 %while.22 = (s32[]{:T(128)}, bf16[5,512,4,64]{1,3,2,0:T(8,128)(2,1)S(1)}, f32[5,4,512]{2,1,0:T(4,128)}, bf16[5,512,3,4,64]{1,4,3,2,0:T(8,128)(2,1)}, s32[5]{0:T(128)S(1)}, /*index=5*/s32[]{:T(128)}) while((s32[]{:T(128)}, bf16[5,512,4,64]{1,3,2,0:T(8,128)(2,1)S(1)}, f32[5,4,512]{2,1,0:T(4,128)}, bf16[5,512,3,4,64]{1,4,3,2,0:T(8,128)(2,1)}, ...), condition=%wide.region_4.5_spmd, body=%wide.region_1.4_spmd.sunk | while | flops 281147904 | bytes 15272541 | solution.py:161
  178.9 5.6 fusion.61
  185.4 176.6 %reduce-scatter.15.cloned.1.call-done = f32[640,1024]{1,0:T(8,128)} async-done(((f32[2560,1024]{1,0:T(8,128)}), f32[640,1024]{1,0:T(8,128)}) %reduce-scatter.15.cloned.1.call-update) | async-done | bytes 2621456 | tf_op jit(solution)/shard_map/reduce_scatter | solution.py:166
  362.0 2.9 fusion.59
  365.4 1.5 fusion.45
  367.6 8.9 all-gather.1
  376.6 16.5 %all-gather.13.cloned.1.call-done = bf16[1024,1024]{1,0:T(8,128)(2,1)} async-done(((bf16[1024,128]{1,0:T(8,128)(2,1)}), bf16[1024,1024]{1,0:T(8,128)(2,1)}) %all-gather.13.cloned.1.call-update) | async-done | bytes 2097168 | tf_op jit(solution)/shard_map/all_gather | solution.py:122
  393.1 100.1 %all-gather.11.cloned.1.call-done = bf16[2560,1024]{1,0:T(8,128)(2,1)} async-done(((bf16[640,1024]{1,0:T(8,128)(2,1)}), bf16[2560,1024]{1,0:T(8,128)(2,1)}) %all-gather.11.cloned.1.call-update) | async-done | bytes 5242896 | tf_op jit(solution)/shard_map/all_gather | solution.py:176
  493.1 32.2 %multiply_convert_fusion.1 = (bf16[2560,1024]{1,0:T(8,128)(2,1)}, f32[2560,1024]{1,0:T(8,128)}, f32[2560,1024]{1,0:T(8,128)}) fusion(f32[1024]{0:T(1024)S(1)} %bitcast.195, bf16[2560,1024]{1,0:T(8,128)(2,1)} %all-gather.11.cloned.1.call-done, bf16[1024,1024]{1,0:T(8,128)(2,1)} %all-gather.13.cloned.1.call-done), kind=kOutput, calls=%fused_computation.56 | convolution fusion | flops 5541724160 | bytes 33558528 | tf_op jit(solution)/shard_map/dot_general | solution.py:31
  525.3 10.2 convolution_convert_fusion.1
  535.8 92.0 %reduce-scatter.17.cloned.1.call-done = bf16[640,1024]{1,0:T(8,128)(2,1)} async-done(((bf16[2560,1024]{1,0:T(8,128)(2,1)}), bf16[640,1024]{1,0:T(8,128)(2,1)}) %reduce-scatter.17.cloned.1.call-update) | async-done | bytes 1310736 | tf_op jit(solution)/shard_map/reduce_scatter | solution.py:181
  627.8 2.3 fusion.57
  632.1 2.1 fusion.56
  635.7 1.9 convert_reduce_fusion.3
  637.8 98.7 %all-gather.17.cloned.1.call-done = bf16[2560,1024]{1,0:T(8,128)(2,1)} async-done(((bf16[640,1024]{1,0:T(8,128)(2,1)}), bf16[2560,1024]{1,0:T(8,128)(2,1)}) %all-gather.17.cloned.1.call-update) | async-done | bytes 5242896 | tf_op jit(solution)/shard_map/all_gather | solution.py:196
  736.4 16.5 %convert_reduce_fusion = (f32[1024]{0:T(1024)S(1)}, bf16[2560,1024]{1,0:T(8,128)(2,1)S(1)}) fusion(f32[2560,1024]{1,0:T(8,128)} %get-tuple-element.266, f32[2560,1024]{1,0:T(8,128)} %get-tuple-element.278, f32[1024]{0:T(1024)S(1)} %bitcast.196, bf16[2560,1024]{1,0:T(8,128)(2,1)} %all-gather.17.cloned.1.call-done, ...), kind=kOutput, calls=%fused_computation.54 | convolution fusion | flops 5413272576 | bytes 33562624 | tf_op jit(solution)/shard_map/dot_general | solution.py:31
  753.0 2.4 copy-done.27
  755.4 7.3 convolution_convert_fusion
  762.7 92.2 %reduce-scatter.19.cloned.1.call-done = bf16[640,1024]{1,0:T(8,128)(2,1)} async-done(((bf16[2560,1024]{1,0:T(8,128)(2,1)}), bf16[640,1024]{1,0:T(8,128)(2,1)}) %reduce-scatter.19.cloned.1.call-update) | async-done | bytes 1310736 | tf_op jit(solution)/shard_map/reduce_scatter | solution.py:202
  855.0 3.5 multiply_reduce_fusion.1
  863.4 97.8 %all-gather.19.cloned.1.call-done = bf16[2560,1024]{1,0:T(8,128)(2,1)} async-done(((bf16[640,1024]{1,0:T(8,128)(2,1)}), bf16[2560,1024]{1,0:T(8,128)(2,1)}) %all-gather.19.cloned.1.call-update) | async-done | bytes 5242896 | tf_op jit(solution)/shard_map/all_gather | solution.py:211
  961.2 5.1 convolution_convert_fusion.2
  966.3 4.3 reshape.259
  970.6 3.0 copy.99
  973.7 60.0 %while.23 = (s32[]{:T(128)}, bf16[5,512,3,4,64]{1,4,3,2,0:T(8,128)(2,1)}, bf16[5,512,3,4,64]{1,4,3,2,0:T(8,128)(2,1)}, s32[5]{0:T(128)S(1)}, f32[5,4,512]{2,1,0:...) while((s32[]{:T(128)}, bf16[5,512,3,4,64]{1,4,3,2,0:T(8,128)(2,1)}, ...), condition=%wide.region_18.19_spmd, body=%wide.region_16.18_spmd.sunk | while | flops 689830400 | bytes 37285476 | solution.py:214
  977.5 2.4 multiply_reduce_fusion.7
  982.6 2.1 fusion.112
  989.5 2.4 multiply_reduce_fusion.7
  994.6 2.1 fusion.112
  1001.6 2.4 multiply_reduce_fusion.7
  1006.6 2.1 fusion.112
  1013.5 2.4 multiply_reduce_fusion.7
  1018.6 2.1 fusion.112
  1025.5 2.4 multiply_reduce_fusion.7
  1030.6 2.1 fusion.112
  1033.6 2.7 convert_reduce_fusion.1
  1036.4 7.7 copy.100
  1044.9 9.7 reshape.240
  1054.8 9.7 convolution_bitcast_fusion
  1064.6 8.3 bitcast_convert_fusion
  1072.9 10.5 fusion.64
  1083.5 10.5 fusion.63
  1094.1 5.9 fusion.62
  1102.8 33.2 %reduce-scatter.23.cloned.1.call-done = f32[3,128,256]{1,2,0:T(8,128)} async-done(((f32[3,1024,256]{1,2,0:T(8,128)}), f32[3,128,256]{1,2,0:T(8,128)}) %reduce-scatter.23.cloned.1.call-update) | async-done | bytes 393232 | tf_op jit(solution)/shard_map/reduce_scatter | solution.py:251
  1135.9 1.9 copy.102
  1137.9 94.2 %reduce-scatter.21.cloned.1.call-done = bf16[640,1024]{1,0:T(8,128)(2,1)} async-done(((bf16[2560,1024]{1,0:T(8,128)(2,1)}), bf16[640,1024]{1,0:T(8,128)(2,1)}) %reduce-scatter.21.cloned.1.call-update) | async-done | bytes 1310736 | tf_op jit(solution)/shard_map/reduce_scatter | solution.py:233
  1232.1 3.4 fusion.54
  1235.5 41.5 %all-reduce.8 = (f32[1024]{0:T(1024)S(1)}, f32[1024]{0:T(1024)S(1)}, f32[1024]{0:T(1024)S(1)}, f32[1024]{0:T(1024)S(1)}, f32[1024]{0:T(1024)S(1)}, /*index=5*/f3...) all-reduce(f32[1024]{0:T(1024)S(1)} %get-tuple-element.220, ...), channel_id=6, replica_groups=mesh['dp'=8,'mp'=4] {'dp','mp'}, use_global_device_ids=true, to_apply=%region_21.22.clone | all-reduce | flops 8192 | bytes 65536
  1281.7 6.0 reduce-scatter.29.cloned.1.call-done
  1287.6 54.8 %reduce-scatter.27.cloned.1.call-done = f32[1024,128]{1,0:T(8,128)} async-done(((f32[1024,1024]{1,0:T(8,128)}), f32[1024,128]{1,0:T(8,128)}) %reduce-scatter.27.cloned.1.call-update) | async-done | bytes 524304 | tf_op jit(solution)/shard_map/reduce_scatter | solution.py:254
  1342.5 39.6 %reduce-scatter.25.cloned.1.call-done = f32[256,128]{1,0:T(8,128)} async-done(((f32[256,1024]{1,0:T(8,128)}), f32[256,128]{1,0:T(8,128)}) %reduce-scatter.25.cloned.1.call-update) | async-done | bytes 131088 | tf_op jit(solution)/shard_map/reduce_scatter | solution.py:252
  (220 shorter events, 93.5 us)
Async XLA Ops:
  7.2 50.4 %copy-start.4 = (bf16[640,1024]{1,0:T(8,128)(2,1)S(1)}, bf16[640,1024]{1,0:T(8,128)(2,1)}, u32[]{:S(2)}) copy-start(bf16[640,1024]{1,0:T(8,128)(2,1)} %param.22) | copy-start | bytes 3932164
  7.2 104.5 %all-gather.9.cloned.1.call-start = ((), (), s32[]{:S(2)}) async-start(), calls=%async_computation.10 | async-start | bytes 1769472 | tf_op jit(solution)/shard_map/all_gather | solution.py:119
  8.1 353.9 %copy-start.9 = (f32[640]{0:T(1024)}, f32[640]{0:T(1024)S(1)}, u32[]{:S(2)}) copy-start(f32[640]{0:T(1024)S(1)} %select_reduce_fusion) | copy-start | bytes 7684
  10.9 35.0 %collective-permute-start = (bf16[640,1024]{1,0:T(8,128)(2,1)}, bf16[640,1024]{1,0:T(8,128)(2,1)S(1)}, u32[]{:S(2)}, u32[]{:S(2)}) collective-permute-start(bf16[640,1024]{1,0:T(8,128)(2,1)} %fusion.44), channel_id=1, source_target_pairs={{0,1},{1,2},{2,3},{3,0},{4,5},{5,6},{6,7},{7,4},{8,9},{9,10},{10,1... | collective-permute-start | bytes 3932168 | tf_op jit(solution)/shard_map/ppermute | solution.py:141
  14.0 348.0 %reduce-scatter.15.cloned.1.call-start = ((), (), s32[]{:S(2)}) async-start(), calls=%async_computation.11 | async-start | bytes 13107200 | tf_op jit(solution)/shard_map/reduce_scatter | solution.py:166
  14.1 59.1 %collective-permute-start.2 = (bf16[640,1024]{1,0:T(8,128)(2,1)}, bf16[640,1024]{1,0:T(8,128)(2,1)}, u32[]{:S(2)}, u32[]{:S(2)}) collective-permute-start(bf16[640,1024]{1,0:T(8,128)(2,1)} %fusion.44), channel_id=1, source_target_pairs={{1,0},{2,1},{3,2},{0,3},{5,4},{6,5},{7,6},{4,7},{9,8},{10,9},{11,1... | collective-permute-start | bytes 3932168 | tf_op jit(solution)/shard_map/ppermute | solution.py:143
  45.9 55.4 %collective-permute-start.1 = (bf16[640,1024]{1,0:T(8,128)(2,1)S(1)}, bf16[640,1024]{1,0:T(8,128)(2,1)}, u32[]{:S(2)}, u32[]{:S(2)}) collective-permute-start(bf16[640,1024]{1,0:T(8,128)(2,1)S(1)} %collective-permute-done), channel_id=1, source_target_pairs={{0,1},{1,2},{2,3},{3,0},{4,5},{5,6},{6,7},{7,4},{8,9},{9,10},{10,1... | collective-permute-start | bytes 3932168 | tf_op jit(solution)/shard_map/ppermute | solution.py:141
  133.1 12.1 copy-start.8
  176.4 8.0 copy-start.25
  177.8 1.1 copy-start.5
  184.4 177.6 %copy-start.12 = (f32[1024]{0:T(1024)S(1)}, f32[1024]{0:T(1024)}, u32[]{:S(2)}) copy-start(f32[1024]{0:T(1024)} %param.26) | copy-start | bytes 12292
  184.4 177.6 %copy-start.13 = (f32[1024]{0:T(1024)S(1)}, f32[1024]{0:T(1024)}, u32[]{:S(2)}) copy-start(f32[1024]{0:T(1024)} %param.25) | copy-start | bytes 12292
  184.4 177.6 %copy-start.21 = (f32[1024]{0:T(1024)S(1)}, f32[1024]{0:T(1024)}, u32[]{:S(2)}) copy-start(f32[1024]{0:T(1024)} %param.30) | copy-start | bytes 12292
  184.4 208.6 %all-gather.13.cloned.1.call-start = ((), (), s32[]{:S(2)}) async-start(), calls=%async_computation.13 | async-start | bytes 2359296 | tf_op jit(solution)/shard_map/all_gather | solution.py:122
  185.2 180.2 %copy-start.11 = (f32[1024]{0:T(1024)S(1)}, f32[1024]{0:T(1024)}, u32[]{:S(2)}) copy-start(f32[1024]{0:T(1024)} %param.31) | copy-start | bytes 12292
  185.2 180.2 %copy-start.14 = (f32[1024]{0:T(1024)S(1)}, f32[1024]{0:T(1024)}, u32[]{:S(2)}) copy-start(f32[1024]{0:T(1024)} %param.32) | copy-start | bytes 12292
  185.2 307.9 %all-gather.11.cloned.1.call-start = ((), (), s32[]{:S(2)}) async-start(), calls=%async_computation.12 | async-start | bytes 6553600 | tf_op jit(solution)/shard_map/all_gather | solution.py:176
  364.9 2.6 copy-start.22
  366.9 158.4 %all-gather.15.cloned.1.call-start = ((), (), s32[]{:S(2)}) async-start(), calls=%async_computation.14 | async-start | bytes 2359296 | tf_op jit(solution)/shard_map/all_gather | solution.py:123
  367.5 260.3 %reduce-scatter.17.cloned.1.call-start = ((), (), s32[]{:S(2)}) async-start(), calls=%async_computation.15 | async-start | bytes 6553600 | tf_op jit(solution)/shard_map/reduce_scatter | solution.py:181
  535.5 92.3 %copy-start.19 = (f32[1024]{0:T(1024)S(1)}, f32[1024]{0:T(1024)}, u32[]{:S(2)}) copy-start(f32[1024]{0:T(1024)} %param.36) | copy-start | bytes 12292
  535.6 95.0 %copy-start.15 = (f32[1024]{0:T(1024)S(1)}, f32[1024]{0:T(1024)}, u32[]{:S(2)}) copy-start(f32[1024]{0:T(1024)} %param.37) | copy-start | bytes 12292
  535.6 200.8 %all-gather.17.cloned.1.call-start = ((), (), s32[]{:S(2)}) async-start(), calls=%async_computation.16 | async-start | bytes 6553600 | tf_op jit(solution)/shard_map/all_gather | solution.py:196
  627.8 2.8 copy-start.6
  630.2 1.9 copy-start.20
  634.3 1.5 copy-start
  637.7 217.2 %reduce-scatter.19.cloned.1.call-start = ((), (), s32[]{:S(2)}) async-start(), calls=%async_computation.17 | async-start | bytes 6553600 | tf_op jit(solution)/shard_map/reduce_scatter | solution.py:202
  736.4 19.0 %copy-start.23 = (bf16[1024,1024]{1,0:T(8,128)(2,1)S(1)}, bf16[1024,1024]{1,0:T(8,128)(2,1)}, u32[]{:S(2)}) copy-start(bf16[1024,1024]{1,0:T(8,128)(2,1)} %all-gather.13.cloned.1.call-done) | copy-start | bytes 6291460
  753.0 2.4 copy-start.27
  762.7 198.5 %all-gather.19.cloned.1.call-start = ((), (), s32[]{:S(2)}) async-start(), calls=%async_computation.18 | async-start | bytes 6553600 | tf_op jit(solution)/shard_map/all_gather | solution.py:211
  855.0 3.5 copy-start.1
  855.0 3.5 copy-start.7
  859.6 1.5 copy-start.2
  862.5 237.6 %reduce-scatter.33.cloned.1.call-start = ((), (), s32[]{:S(2)}) async-start(), calls=%async_computation.25 | async-start | bytes 73728
  863.3 238.1 %reduce-scatter.31.cloned.1.call-start = ((), (), s32[]{:S(2)}) async-start(), calls=%async_computation.24 | async-start | bytes 73728
  966.3 7.3 copy-start.26
  1054.6 10.0 copy-start.24
  1054.6 81.3 %reduce-scatter.23.cloned.1.call-start = ((), (), s32[]{:S(2)}) async-start(), calls=%async_computation.20 | async-start | bytes 3538944 | tf_op jit(solution)/shard_map/reduce_scatter | solution.py:251
  1064.5 167.5 %reduce-scatter.21.cloned.1.call-start = ((), (), s32[]{:S(2)}) async-start(), calls=%async_computation.19 | async-start | bytes 6553600 | tf_op jit(solution)/shard_map/reduce_scatter | solution.py:233
  1072.9 214.8 %reduce-scatter.29.cloned.1.call-start = ((), (), s32[]{:S(2)}) async-start(), calls=%async_computation.23 | async-start | bytes 4718592 | tf_op jit(solution)/shard_map/reduce_scatter | solution.py:255
  1083.4 259.0 %reduce-scatter.27.cloned.1.call-start = ((), (), s32[]{:S(2)}) async-start(), calls=%async_computation.22 | async-start | bytes 4718592 | tf_op jit(solution)/shard_map/reduce_scatter | solution.py:254
  1094.0 138.1 %copy-start.3 = (f32[640,1024]{1,0:T(8,128)S(1)}, f32[640,1024]{1,0:T(8,128)}, u32[]{:S(2)}) copy-start(f32[640,1024]{1,0:T(8,128)} %copy-done.2) | copy-start | bytes 7864324
  1094.0 138.1 %copy-start.10 = (f32[640]{0:T(1024)S(1)}, f32[640]{0:T(1024)}, u32[]{:S(2)}) copy-start(f32[640]{0:T(1024)} %copy-done.9) | copy-start | bytes 7684
  1094.0 288.1 %reduce-scatter.25.cloned.1.call-start = ((), (), s32[]{:S(2)}) async-start(), calls=%async_computation.21 | async-start | bytes 1179648 | tf_op jit(solution)/shard_map/reduce_scatter | solution.py:252
  1100.0 135.5 %copy-start.16 = (f32[1024]{0:T(1024)S(1)}, f32[1024]{0:T(1024)}, u32[]{:S(2)}) copy-start(f32[1024]{0:T(1024)} %get-tuple-element.216) | copy-start | bytes 12292
  1100.0 135.5 %copy-start.17 = (f32[1024]{0:T(1024)S(1)}, f32[1024]{0:T(1024)}, u32[]{:S(2)}) copy-start(f32[1024]{0:T(1024)} %get-tuple-element.221) | copy-start | bytes 12292
  1100.0 135.5 %copy-start.18 = (f32[1024]{0:T(1024)S(1)}, f32[1024]{0:T(1024)}, u32[]{:S(2)}) copy-start(f32[1024]{0:T(1024)} %get-tuple-element.254) | copy-start | bytes 12292
Sparse Core Ops, SparseCore 0:
  14.1 25.7 all-gather.8
  184.6 177.3 reduce-scatter.14
  363.9 29.1 all-gather.12
  395.1 98.0 all-gather.10
  494.9 26.4 all-gather.14
  535.7 92.0 reduce-scatter.16
  637.8 98.5 all-gather.16
  762.8 92.0 reduce-scatter.18
  862.6 98.5 all-gather.18
  964.0 31.8 reduce-scatter.32
  1054.7 31.8 reduce-scatter.30
  1089.9 46.0 reduce-scatter.22
  1138.2 93.7 reduce-scatter.20
  1235.8 51.7 reduce-scatter.28
  1291.4 51.0 reduce-scatter.26
  1346.1 35.9 reduce-scatter.24
